TPU v7x, 256 devices: a whole 4x4x8 slice. The times are simulated.
256 devices in a mesh: dp: 16 (over x_lo, y, core), mp: 8 (over z), side: 2 (over x_hi).
Axes of the slice: x: 4 (x_hi: 2, x_lo: 2; x = x_hi * 2 + x_lo), y: 4, z: 8, core: 2. Of those that a mesh axis runs over, the one named last changes fastest.
Arguments:
- tokens: bfloat16 [4096, 3072], P('dp', 'mp'), may hold values from -6 to 6
- up_weight: bfloat16 [2, 3072, 6144], P('side', 'dp', 'mp'), may hold values from -0.109375 to 0.109375
- down_weight: bfloat16 [2, 6144, 3072], P('side', 'mp', 'dp'), may hold values from -0.078125 to 0.078125
- mod_table: float32 [2, 50, 3, 3072], P('side'), may hold values from -3 to 3
- timesteps: int32 [16], P('dp'), may hold values from 0 to 49
- valid_counts: int32 [16], replicated, may hold values from 64 to 256, as said below
Outputs:
- block_out: bfloat16 [2, 4096, 3072], P('side', 'dp', 'mp')
- up_grads: float32 [3072, 6144], P(('dp', 'side'), 'mp')
- down_grads: float32 [6144, 3072], P('mp', ('dp', 'side'))
Inputs may be any that keep to these rules, and one draw needn't show every extreme that they name: `valid_counts`: every image has at least 64 valid tokens, and in every draw some image has all 256 valid.
All inputs are finite; a program needn't handle non-finite values.
Results may differ from a plain program's by a relative error of at most 0.018.
Values may be sent and summed in bfloat16 or wider, within the bound.
A program may use at most 64 MiB of HBM per device.

v0:
```python
import jax
import jax.numpy as jnp
from jax import lax
from jax.sharding import PartitionSpec as P


def passed_along(x, axis, by):
    peers = lax.axis_size(axis)
    pairs = [(i, i + by) for i in range(peers) if 0 <= i + by < peers]
    return lax.ppermute(x, axis, pairs)


def gelu_tanh(values):
    return jax.nn.gelu(values, approximate=True)


def shards(tokens, up_weight, down_weight, mod_table, timesteps, valid_counts):
    gathered = lax.all_gather(tokens, "mp", axis=1, tiled=True)
    width = gathered.shape[1]
    shard_width = tokens.shape[1]
    mp_offset = lax.axis_index("mp") * shard_width
    is_student = lax.axis_index("side") == 1
    wide = gathered.astype(jnp.float32)
    average = jnp.mean(wide, axis=-1, keepdims=True)
    centred = wide - average
    variance = jnp.mean(centred * centred, axis=-1, keepdims=True)
    scaled = centred * lax.rsqrt(variance + 1e-06)
    plan = mod_table.shape[1]
    one_hot = (jnp.arange(plan, dtype=jnp.int32)[None, :] == timesteps[0]).astype(jnp.float32)
    modulation = jnp.dot(
        one_hot,
        mod_table[0].reshape(plan, 3 * width),
        precision=lax.Precision.HIGHEST,
        preferred_element_type=jnp.float32,
    ).reshape(3, width)
    normed = (scaled * (1.0 + modulation[1]) + modulation[0]).astype(jnp.bfloat16)
    gate_row = modulation[2]
    hidden_pre = jnp.dot(
        normed,
        lax.all_gather(up_weight[0], "dp", axis=0, tiled=True),
        preferred_element_type=jnp.float32,
    )
    hidden_act = gelu_tanh(hidden_pre).astype(jnp.bfloat16)
    down_full = lax.all_gather(down_weight[0], "dp", axis=1, tiled=True)
    partial_value = jnp.dot(hidden_act, down_full, preferred_element_type=jnp.float32)
    positions = jnp.arange(normed.shape[0], dtype=jnp.int32)
    own_count = lax.dynamic_index_in_dim(valid_counts, lax.axis_index("dp"), 0, keepdims=False)
    valid_col = (positions < own_count).astype(jnp.float32)[:, None]
    valid_total = jnp.sum(valid_counts).astype(jnp.float32)
    mixed = lax.psum(partial_value.astype(jnp.bfloat16), "mp").astype(jnp.float32)
    out_full = (wide + gate_row * mixed).astype(jnp.bfloat16)
    out_local = lax.dynamic_slice_in_dim(out_full, mp_offset, shard_width, 1)
    other_full = passed_along(out_full, "side", 1)
    differ = out_full.astype(jnp.float32) - other_full.astype(jnp.float32)
    grad_out = (gate_row * differ * valid_col / jnp.sqrt(valid_total)).astype(jnp.bfloat16)

    def backprop():
        grad_act = lax.dot_general(
            grad_out, down_full, (((1,), (1,)), ((), ())), preferred_element_type=jnp.float32
        )
        unused, pullback = jax.vjp(gelu_tanh, hidden_pre)
        return pullback(grad_act)[0].astype(jnp.bfloat16)

    def no_backprop():
        return jnp.zeros(hidden_pre.shape, jnp.bfloat16)

    grad_pre = lax.cond(is_student, backprop, no_backprop)
    ff_width = hidden_act.shape[1]

    def product():
        return lax.dot_general(
            normed, grad_pre, (((0,), (0,)), ((), ())), preferred_element_type=jnp.float32
        )

    def nothing():
        return jnp.zeros(
            (width // lax.axis_size(("dp", "side")) * lax.axis_size(("dp", "side")), ff_width),
            jnp.float32,
        )

    up_share = lax.psum_scatter(
        lax.cond(is_student, product, nothing).astype(jnp.bfloat16),
        ("dp", "side"),
        scatter_dimension=0,
        tiled=True,
    ).astype(jnp.float32)

    def down_product():
        return lax.dot_general(
            hidden_act, grad_out, (((0,), (0,)), ((), ())), preferred_element_type=jnp.float32
        )

    def down_nothing():
        return jnp.zeros((ff_width, width), jnp.float32)

    down_term = lax.cond(is_student, down_product, down_nothing)
    down_share = lax.psum_scatter(
        down_term.astype(jnp.bfloat16), ("dp", "side"), scatter_dimension=1, tiled=True
    ).astype(jnp.float32)
    return (out_local[None], up_share, down_share)


def solution(mesh):
    placed = (
        P("dp", "mp"),
        P("side", "dp", "mp"),
        P("side", "mp", "dp"),
        P("side", None, None, None),
        P("dp"),
        P(),
    )
    return jax.shard_map(
        shards,
        mesh=mesh,
        in_specs=placed,
        out_specs=(P("side", "dp", "mp"), P(("dp", "side"), "mp"), P("mp", ("dp", "side"))),
        check_vma=False,
    )
```

profile of v0, /device:TPU:1, one launch (start us, length us, event | category | flops | bytes accessed | tf_op | source)
XLA Modules:
  0.0 593.4 jit_solution(2284106600337096998)
XLA Ops:
  7.2 0.0 all-gather.6.cloned.1.call-start
  7.2 0.7 all-gather.6.cloned.1.call-update
  7.9 0.0 all-gather.8.cloned.1.call-start
  7.9 0.7 all-gather.8.cloned.1.call-update
  8.6 0.0 all-gather.10.cloned.1.call-start
  8.7 0.7 all-gather.10.cloned.1.call-update
  9.4 0.0 all-reduce.2.cloned.1.call-start
  9.4 6.5 %reduce = f32[50,3,3072]{2,1,0:T(4,128)S(1)} reduce(f32[1,50,3,3072]{3,0,2,1:T(1,128)} %param.15, f32[]{:T(128)} %constant.65), dimensions={0}, to_apply=%param.15.reduce_sub_computation | reduce | bytes 3686404 | tf_op args[3]
  15.9 0.5 pad
  16.5 1.2 copy.14
  18.3 0.8 fusion.24
  19.1 29.2 %all-gather.6.cloned.1.call-done = bf16[256,3072]{1,0:T(8,128)(2,1)} async-done(((bf16[256,384]{1,0:T(8,128)(2,1)}), bf16[256,3072]{1,0:T(8,128)(2,1)}) %all-gather.6.cloned.1.call-update) | async-done | bytes 1572880 | tf_op jit(solution)/shard_map/all_gather | solution.py:18
  48.2 0.0 copy-start
  48.2 1.8 convert_reduce_fusion
  50.1 2.0 fusion.11
  52.0 0.0 copy-done
  52.0 0.8 fusion.14
  52.8 41.7 %all-gather.8.cloned.1.call-done = bf16[1,3072,768]{2,1,0:T(8,128)(2,1)} async-done(((bf16[1,192,768]{2,1,0:T(8,128)(2,1)}), bf16[1,3072,768]{2,1,0:T(8,128)(2,1)}) %all-gather.8.cloned.1.call-update) | async-done | bytes 4718608 | tf_op jit(solution)/shard_map/all_gather | solution.py:40
  94.5 4.6 fusion.23
  99.2 37.7 %all-gather.10.cloned.1.call-done = bf16[1,768,3072]{1,2,0:T(8,128)(2,1)} async-done(((bf16[1,768,192]{1,2,0:T(8,128)(2,1)}), bf16[1,768,3072]{1,2,0:T(8,128)(2,1)}) %all-gather.10.cloned.1.call-update) | async-done | bytes 4718608 | tf_op jit(solution)/shard_map/all_gather | solution.py:44
  136.9 4.9 convolution_convert_fusion
  141.8 0.0 copy-done.1
  141.8 0.0 all-reduce.2.cloned.1.call-update
  141.8 0.2 reduce-scatter.3.cloned.1.call-start
  142.1 74.3 %all-reduce.2.cloned.1.call-done = bf16[256,3072]{1,0:T(8,128)(2,1)} async-done(((bf16[256,3072]{1,0:T(8,128)(2,1)}), bf16[256,3072]{1,0:T(8,128)(2,1)}) %all-reduce.2.cloned.1.call-update) | async-done | bytes 1572880 | tf_op jit(solution)/shard_map/psum | solution.py:50
  216.3 3.1 fusion.15
  219.5 5.8 collective-permute-start
  225.2 0.0 copy-done.3
  225.2 0.6 reduce_sum.29
  226.6 0.6 dynamic_slice.8
  227.2 0.6 compare_convert_fusion
  227.8 25.6 %collective-permute-done = bf16[256,3072]{1,0:T(8,128)(2,1)} collective-permute-done((bf16[256,3072]{1,0:T(8,128)(2,1)}, bf16[256,3072]{1,0:T(8,128)(2,1)}, u32[]{:S(2)}, u32[]{:S(2)}) %collective-permute-start) | collective-permute-done | bytes 1572896 | tf_op jit(solution)/shard_map/ppermute | solution.py:10
  253.4 2.6 divide_convert_fusion
  256.0 0.1 conditional.3
  256.1 2.5 conditional.4
  256.1 2.5 broadcast.75
  258.6 0.0 reduce-scatter.3.cloned.1.call-update
  258.6 0.0 reduce-scatter.5.cloned.1.call-start
  258.6 0.9 copy-done.2
  259.6 2.8 conditional.5
  259.6 2.8 broadcast.76
  262.4 6.6 %copy.12 = bf16[768,3072]{0,1:T(8,128)(2,1)} copy(bf16[768,3072]{1,0:T(8,128)(2,1)} %get-tuple-element.43) | data formatting | bytes 9437184 | tf_op jit(solution)/shard_map/cond | solution.py:96
  269.0 0.0 reduce-scatter.5.cloned.1.call-update
  269.0 1.6 dynamic-slice_bitcast_fusion
  270.6 155.2 %reduce-scatter.3.cloned.1.call-done = bf16[96,768]{1,0:T(8,128)(2,1)} async-done(((bf16[3072,768]{1,0:T(8,128)(2,1)}), bf16[96,768]{1,0:T(8,128)(2,1)}) %reduce-scatter.3.cloned.1.call-update) | async-done | bytes 147472 | tf_op jit(solution)/shard_map/reduce_scatter | solution.py:81
  425.9 1.6 convert_element_type.71
  427.5 157.4 %reduce-scatter.5.cloned.1.call-done = bf16[768,96]{0,1:T(8,128)(2,1)} async-done(((bf16[768,3072]{0,1:T(8,128)(2,1)}), bf16[768,96]{0,1:T(8,128)(2,1)}) %reduce-scatter.5.cloned.1.call-update) | async-done | bytes 147472 | tf_op jit(solution)/shard_map/reduce_scatter | solution.py:97
  584.9 1.6 convert_element_type.73
  (7 shorter events, 0.1 us)
Async XLA Ops:
  7.2 41.1 %all-gather.6.cloned.1.call-start = ((), (), s32[]{:S(2)}) async-start(), calls=%async_computation.2 | async-start | bytes 1769472 | tf_op jit(solution)/shard_map/all_gather | solution.py:18
  7.9 86.6 %all-gather.8.cloned.1.call-start = ((), (), s32[]{:S(2)}) async-start(), calls=%async_computation.6 | async-start | bytes 5013504 | tf_op jit(solution)/shard_map/all_gather | solution.py:40
  8.6 128.2 %all-gather.10.cloned.1.call-start = ((), (), s32[]{:S(2)}) async-start(), calls=%async_computation.7 | async-start | bytes 5013504 | tf_op jit(solution)/shard_map/all_gather | solution.py:44
  9.4 207.0 %all-reduce.2.cloned.1.call-start = ((), (), s32[]{:S(2)}) async-start(), calls=%async_computation.3 | async-start | bytes 3145728 | tf_op jit(solution)/shard_map/psum | solution.py:50
  48.2 3.8 copy-start
  99.2 42.7 %copy-start.1 = (bf16[256,768]{1,0:T(8,128)(2,1)}, bf16[256,768]{1,0:T(8,128)(2,1)S(1)}, u32[]{:S(2)}) copy-start(bf16[256,768]{1,0:T(8,128)(2,1)S(1)} %get-tuple-element.39) | copy-start | bytes 1179652
  141.8 83.4 %copy-start.3 = (s32[16]{0:T(128)S(1)}, s32[16]{0:T(128)}, u32[]{:S(2)}) copy-start(s32[16]{0:T(128)} %param.17) | copy-start | bytes 196
  141.8 284.0 %reduce-scatter.3.cloned.1.call-start = ((), (), s32[]{:S(2)}) async-start(), calls=%async_computation.4 | async-start | bytes 4866048 | tf_op jit(solution)/shard_map/reduce_scatter | solution.py:81
  219.5 34.0 %collective-permute-start = (bf16[256,3072]{1,0:T(8,128)(2,1)}, bf16[256,3072]{1,0:T(8,128)(2,1)}, u32[]{:S(2)}, u32[]{:S(2)}) collective-permute-start(bf16[256,3072]{1,0:T(8,128)(2,1)} %fusion.15), channel_id=1, source_target_pairs={{0,1},{2,3},{4,5},{6,7},{8,9},{10,11},{12,13},{14,15},{16,17},{18,... | collective-permute-start | bytes 4718600 | tf_op jit(solution)/shard_map/ppermute | solution.py:10
  258.6 1.0 copy-start.2
  258.6 326.3 %reduce-scatter.5.cloned.1.call-start = ((), (), s32[]{:S(2)}) async-start(), calls=%async_computation.5 | async-start | bytes 4866048 | tf_op jit(solution)/shard_map/reduce_scatter | solution.py:97
Sparse Core Ops, SparseCore 0:
  9.8 38.4 all-gather.5
  50.1 44.3 all-gather.7
  96.4 40.4 all-gather.9
  142.0 74.3 all-reduce.1
  258.7 167.0 reduce-scatter.2
  428.2 156.6 reduce-scatter.4
where the time goes:
time: 594 us; the launch traced here: 593 us
  waiting for transfers between devices  523 us (88%)
  other arithmetic  21.3 us (4%)
  local copies, waits for them, and re-layouts  16.8 us (3%)
  between operations  15.5 us (3%)
  matrix products  10.3 us (2%)
  starting transfers between devices  6.19 us (1%)
    reduce_scatter x1, waiting for transfers between devices, shards(): lax.psum_scatter(down_term.astype(jnp.bfloat16), ('dp', 'side'), scatter_...  157 us
    reduce_scatter x1, waiting for transfers between devices, shards(): lax.psum_scatter(lax.cond(is_student, product, nothing).astype(jnp.bfloat...  155 us
    psum x1, waiting for transfers between devices, shards(): lax.psum(partial_value.astype(jnp.bfloat16), 'mp').astype(jnp.float32)  74.3 us
    all_gather x1, waiting for transfers between devices, shards(): lax.all_gather(up_weight[0], 'dp', axis=0, tiled=True)  41.7 us
    all_gather x1, waiting for transfers between devices, shards(): down_full = lax.all_gather(down_weight[0], 'dp', axis=1, tiled=True)  37.7 us
    all_gather x1, waiting for transfers between devices, shards(): gathered = lax.all_gather(tokens, 'mp', axis=1, tiled=True)  29.2 us
    ppermute x1, waiting for transfers between devices, passed_along(): return lax.ppermute(x, axis, pairs)  25.6 us
  transfers between devices with their start and end apart: 7, of which 7 were waited for; matrix products, arithmetic and copies ran while one was open for 6% of the time, Pallas kernels for 0%

commit v1 on v0

--- a/solution.py
+++ b/solution.py
@@ -2,6 +2,12 @@
 import jax.numpy as jnp
 from jax import lax
 from jax.sharding import PartitionSpec as P
+
+
+def add_all(x, mesh_axis):
+    pieces = lax.all_gather(x, mesh_axis, axis=0, tiled=False)
+    total = pieces.sum(axis=0)
+    return total
 
 
 def passed_along(x, axis, by):
@@ -47,7 +53,7 @@
     own_count = lax.dynamic_index_in_dim(valid_counts, lax.axis_index("dp"), 0, keepdims=False)
     valid_col = (positions < own_count).astype(jnp.float32)[:, None]
     valid_total = jnp.sum(valid_counts).astype(jnp.float32)
-    mixed = lax.psum(partial_value.astype(jnp.bfloat16), "mp").astype(jnp.float32)
+    mixed = add_all(partial_value.astype(jnp.bfloat16), "mp").astype(jnp.float32)
     out_full = (wide + gate_row * mixed).astype(jnp.bfloat16)
     out_local = lax.dynamic_slice_in_dim(out_full, mp_offset, shard_width, 1)
     other_full = passed_along(out_full, "side", 1)

time: 594 us -> 662 us (1.11)
  waiting for transfers between devices: 523 us -> 584 us
  other arithmetic: 21.3 us -> 30.2 us
    all_gather x0 -> x1, waiting for transfers between devices: none -> 133 us  [add_all(): pieces = lax.all_gather(x, mesh_axis, axis=0, tiled=False)]
    psum x1 -> x0, waiting for transfers between devices: 74.3 us -> none  [shards(): lax.psum(partial_value.astype(jnp.bfloat16), 'mp').astype(jnp.float32)]
    reduce_sum x0 -> x1, other arithmetic: none -> 8.76 us  [add_all(): total = pieces.sum(axis=0)]
  transfers between devices with their start and end apart: 7 -> 7, of which waited for: 7 -> 7; matrix products, arithmetic and copies ran while one was open for 6% -> 4% of each run, Pallas kernels for 0% -> 0%
where the time goes in v1:
time: 662 us
  waiting for transfers between devices  584 us (88%)
  other arithmetic  30.2 us (5%)
  local copies, waits for them, and re-layouts  15.8 us (2%)
  between operations  15.5 us (2%)
  matrix products  10.3 us (2%)
    reduce_scatter x1, waiting for transfers between devices, shards(): lax.psum_scatter(lax.cond(is_student, product, nothing).astype(jnp.bfloat...  157 us
    reduce_scatter x1, waiting for transfers between devices, shards(): lax.psum_scatter(down_term.astype(jnp.bfloat16), ('dp', 'side'), scatter_...  154 us
    all_gather x1, waiting for transfers between devices, add_all(): pieces = lax.all_gather(x, mesh_axis, axis=0, tiled=False)  133 us
    all_gather x1, waiting for transfers between devices, shards(): lax.all_gather(up_weight[0], 'dp', axis=0, tiled=True)  41.7 us
    all_gather x1, waiting for transfers between devices, shards(): down_full = lax.all_gather(down_weight[0], 'dp', axis=1, tiled=True)  37.7 us
    ppermute x1, waiting for transfers between devices, passed_along(): return lax.ppermute(x, axis, pairs)  29.5 us
    all_gather x1, waiting for transfers between devices, shards(): gathered = lax.all_gather(tokens, 'mp', axis=1, tiled=True)  29.2 us
  transfers between devices with their start and end apart: 7, of which 7 were waited for; matrix products, arithmetic and copies ran while one was open for 4% of the time, Pallas kernels for 0%

profile of v1, /device:TPU:1, one launch (start us, length us, event | category | flops | bytes accessed | tf_op | source)
XLA Modules:
  0.0 661.6 jit_solution(3840718613388631985)
XLA Ops:
  7.2 0.0 all-gather.8.cloned.1.call-start
  7.2 0.7 all-gather.8.cloned.1.call-update
  7.9 0.0 all-gather.10.cloned.1.call-start
  7.9 0.7 all-gather.10.cloned.1.call-update
  8.6 0.0 all-gather.12.cloned.1.call-start
  8.7 0.7 all-gather.12.cloned.1.call-update
  9.4 0.0 all-gather.14.cloned.1.call-start
  9.4 6.5 reduce.1
  15.9 0.5 pad
  16.5 1.2 copy.14
  18.3 0.8 fusion.24
  19.1 29.2 %all-gather.8.cloned.1.call-done = bf16[256,3072]{1,0:T(8,128)(2,1)} async-done(((bf16[256,384]{1,0:T(8,128)(2,1)}), bf16[256,3072]{1,0:T(8,128)(2,1)}) %all-gather.8.cloned.1.call-update) | async-done | bytes 1572880 | tf_op jit(solution)/shard_map/all_gather | solution.py:24
  48.2 0.0 copy-start
  48.2 1.8 convert_reduce_fusion
  50.1 2.0 fusion.11
  52.0 0.0 copy-done
  52.0 0.8 fusion.14
  52.8 41.7 %all-gather.10.cloned.1.call-done = bf16[1,3072,768]{2,1,0:T(8,128)(2,1)} async-done(((bf16[1,192,768]{2,1,0:T(8,128)(2,1)}), bf16[1,3072,768]{2,1,0:T(8,128)(2,1)}) %all-gather.10.cloned.1.call-update) | async-done | bytes 4718608 | tf_op jit(solution)/shard_map/all_gather | solution.py:46
  94.5 4.6 fusion.23
  99.1 37.7 %all-gather.12.cloned.1.call-done = bf16[1,768,3072]{1,2,0:T(8,128)(2,1)} async-done(((bf16[1,768,192]{1,2,0:T(8,128)(2,1)}), bf16[1,768,3072]{1,2,0:T(8,128)(2,1)}) %all-gather.12.cloned.1.call-update) | async-done | bytes 4718608 | tf_op jit(solution)/shard_map/all_gather | solution.py:50
  136.9 4.9 convolution_convert_fusion
  141.8 0.0 all-gather.14.cloned.1.call-update
  141.9 0.2 reduce-scatter.5.cloned.1.call-start
  142.1 132.8 %all-gather.14.cloned.1.call-done = bf16[2048,3072]{1,0:T(8,128)(2,1)} async-done(((bf16[256,3072]{1,0:T(8,128)(2,1)}), bf16[2048,3072]{1,0:T(8,128)(2,1)}) %all-gather.14.cloned.1.call-update) | async-done | bytes 12582928 | tf_op jit(solution)/shard_map/all_gather | solution.py:8
  274.9 8.8 %reduce_sum.41 = bf16[256,3072]{1,0:T(8,128)(2,1)} reduce(bf16[8,256,3072]{2,1,0:T(8,128)(2,1)} %bitcast.31, bf16[]{:T(256)} %constant.53.clone.1), dimensions={0}, to_apply=%region_2.3 | reduce | flops 5505024 | bytes 14155778 | tf_op jit(solution)/shard_map/reduce_sum | solution.py:9
  283.6 0.0 copy-start.1
  283.6 3.2 fusion.15
  286.8 5.7 collective-permute-start
  292.6 0.0 copy-done.1
  292.6 0.6 reduce_sum.42
  293.2 0.6 dynamic_slice.8
  294.5 0.7 compare_convert_fusion
  295.1 29.5 %collective-permute-done = bf16[256,3072]{1,0:T(8,128)(2,1)} collective-permute-done((bf16[256,3072]{1,0:T(8,128)(2,1)}, bf16[256,3072]{1,0:T(8,128)(2,1)}, u32[]{:S(2)}, u32[]{:S(2)}) %collective-permute-start) | collective-permute-done | bytes 1572896 | tf_op jit(solution)/shard_map/ppermute | solution.py:16
  324.6 2.6 divide_convert_fusion
  327.2 2.8 conditional.5
  327.2 2.8 broadcast.76
  330.0 6.6 %copy.12 = bf16[768,3072]{0,1:T(8,128)(2,1)} copy(bf16[768,3072]{1,0:T(8,128)(2,1)} %get-tuple-element.43) | data formatting | bytes 9437184 | tf_op jit(solution)/shard_map/cond | solution.py:102
  336.6 0.0 reduce-scatter.5.cloned.1.call-update
  336.7 0.0 reduce-scatter.3.cloned.1.call-start
  336.7 0.1 conditional.3
  336.8 2.5 conditional.4
  336.8 2.5 broadcast.75
  339.3 0.0 reduce-scatter.3.cloned.1.call-update
  339.3 1.6 dynamic-slice_bitcast_fusion
  340.9 153.5 %reduce-scatter.5.cloned.1.call-done = bf16[768,96]{0,1:T(8,128)(2,1)} async-done(((bf16[768,3072]{0,1:T(8,128)(2,1)}), bf16[768,96]{0,1:T(8,128)(2,1)}) %reduce-scatter.5.cloned.1.call-update) | async-done | bytes 147472 | tf_op jit(solution)/shard_map/reduce_scatter | solution.py:103
  494.4 1.6 convert_element_type.75
  496.1 157.0 %reduce-scatter.3.cloned.1.call-done = bf16[96,768]{1,0:T(8,128)(2,1)} async-done(((bf16[3072,768]{1,0:T(8,128)(2,1)}), bf16[96,768]{1,0:T(8,128)(2,1)}) %reduce-scatter.3.cloned.1.call-update) | async-done | bytes 147472 | tf_op jit(solution)/shard_map/reduce_scatter | solution.py:87
  653.1 1.6 convert_element_type.73
  (4 shorter events, 0.1 us)
Async XLA Ops:
  7.2 41.1 %all-gather.8.cloned.1.call-start = ((), (), s32[]{:S(2)}) async-start(), calls=%async_computation.2 | async-start | bytes 1769472 | tf_op jit(solution)/shard_map/all_gather | solution.py:24
  7.9 86.6 %all-gather.10.cloned.1.call-start = ((), (), s32[]{:S(2)}) async-start(), calls=%async_computation.5 | async-start | bytes 5013504 | tf_op jit(solution)/shard_map/all_gather | solution.py:46
  8.6 128.2 %all-gather.12.cloned.1.call-start = ((), (), s32[]{:S(2)}) async-start(), calls=%async_computation.6 | async-start | bytes 5013504 | tf_op jit(solution)/shard_map/all_gather | solution.py:50
  9.4 265.5 %all-gather.14.cloned.1.call-start = ((), (), s32[]{:S(2)}) async-start(), calls=%async_computation.7 | async-start | bytes 14155776 | tf_op jit(solution)/shard_map/all_gather | solution.py:8
  48.2 3.8 copy-start
  141.9 352.6 %reduce-scatter.5.cloned.1.call-start = ((), (), s32[]{:S(2)}) async-start(), calls=%async_computation.4 | async-start | bytes 4866048 | tf_op jit(solution)/shard_map/reduce_scatter | solution.py:103
  283.6 8.9 %copy-start.1 = (s32[16]{0:T(128)S(1)}, s32[16]{0:T(128)}, u32[]{:S(2)}) copy-start(s32[16]{0:T(128)} %param.17) | copy-start | bytes 196
  286.8 37.8 %collective-permute-start = (bf16[256,3072]{1,0:T(8,128)(2,1)}, bf16[256,3072]{1,0:T(8,128)(2,1)}, u32[]{:S(2)}, u32[]{:S(2)}) collective-permute-start(bf16[256,3072]{1,0:T(8,128)(2,1)} %fusion.15), channel_id=1, source_target_pairs={{0,1},{2,3},{4,5},{6,7},{8,9},{10,11},{12,13},{14,15},{16,17},{18,... | collective-permute-start | bytes 4718600 | tf_op jit(solution)/shard_map/ppermute | solution.py:16
  336.7 316.4 %reduce-scatter.3.cloned.1.call-start = ((), (), s32[]{:S(2)}) async-start(), calls=%async_computation.3 | async-start | bytes 4866048 | tf_op jit(solution)/shard_map/reduce_scatter | solution.py:87
Sparse Core Ops, SparseCore 0:
  9.8 38.4 all-gather.7
  50.1 44.3 all-gather.9
  96.4 40.4 all-gather.11
  142.0 132.8 all-gather.13
  336.8 157.5 reduce-scatter.4
  496.8 156.2 reduce-scatter.2
